TPU v7x, 32 devices: a whole 2x2x4 slice. The times are simulated.
32 devices in a mesh: view: 4 (over y, core), row: 8 (over z, x).
Axes of the slice: x: 2, y: 2, z: 4, core: 2. Of those that a mesh axis runs over, the one named last changes fastest.
Arguments:
- features: float32 [4, 16384, 2048], P('view', 'row'), may hold values from -0.125 to 0.125
- view_maps: float32 [4, 2048, 256], P('view', 'row'), may hold values from -6 to 6
- shared: float32 [16384, 256], P('row'), may hold values from -6 to 6
Outputs:
- maps_out: float32 [4, 2048, 256], P('view', 'row')
- shared_out: float32 [16384, 256], P('row')
All inputs are finite; a program needn't handle non-finite values.
Results may differ from a plain program's by a relative error of at most 0.00013.
Values sent between devices are 32-bit elements; how exact they have to be, the bound alone decides.
A program may use at most 128 MiB of HBM per device.

v0:
```python
import jax
import jax.numpy as jnp
from jax import lax
from jax.sharding import PartitionSpec as P

ITERS = 2
NEWTON = 5
step_rate = 0.5


def newton_root(gram_matrix):
    highest = lax.Precision.HIGHEST
    frob_norm = jnp.sqrt(jnp.sum(gram_matrix * gram_matrix))
    scaled = gram_matrix / frob_norm
    identity = jnp.eye(gram_matrix.shape[0], dtype=jnp.float32)
    inverse_root = identity
    for newton_step in range(NEWTON):
        correction = 1.5 * identity - 0.5 * jnp.dot(inverse_root, scaled, precision=highest)
        scaled = jnp.dot(scaled, correction, precision=highest)
        inverse_root = jnp.dot(correction, inverse_root, precision=highest)
    return (inverse_root, frob_norm)


def local(features, view_maps, shared):
    highest = lax.Precision.HIGHEST
    samples = features[0]
    map_shard = view_maps[0]
    local_rows = samples.shape[0]
    width = samples.shape[1]
    shard_rows = map_shard.shape[0]
    total_rows = local_rows * lax.axis_size("row")
    view_count = lax.axis_size("view")
    step_size = step_rate * width / total_rows
    whole_map = lax.all_gather(map_shard, "row", axis=0, tiled=True)
    projected = jnp.dot(samples, whole_map, precision=highest)
    for iteration in range(ITERS):
        residual = projected - shared
        gradient = lax.psum(jnp.dot(samples.T, residual, precision=highest), "row")
        whole_map = whole_map - step_size * gradient
        projected = jnp.dot(samples, whole_map, precision=highest)
        average = lax.psum(projected, "view") / view_count
        gram_matrix = lax.psum(jnp.dot(average.T, average, precision=highest), "row")
        inverse_root, frob_norm = newton_root(gram_matrix)
        shared = jnp.dot(average, inverse_root, precision=highest) * jnp.sqrt(
            total_rows / frob_norm
        )
    map_shard = lax.dynamic_slice_in_dim(
        whole_map, lax.axis_index("row") * shard_rows, shard_rows, 0
    )
    return (map_shard[None], shared)


def solution(mesh):
    in_specs = (P("view", "row", None), P("view", "row", None), P("row", None))
    out_specs = (P("view", "row", None), P("row", None))
    return jax.shard_map(local, mesh=mesh, in_specs=in_specs, out_specs=out_specs, check_vma=False)
```

profile of v0, /device:TPU:0, one launch (start us, length us, event | category | flops | bytes accessed | tf_op | source)
XLA Modules:
  0.0 663.0 jit_solution(7803501747945105830)
XLA Ops:
  7.2 1.8 copy.6
  9.1 54.6 %all-gather.3.cloned.1.call-done = f32[1,2048,256]{1,2,0:T(8,128)} async-done(((f32[1,256,256]{1,2,0:T(8,128)}), f32[1,2048,256]{1,2,0:T(8,128)}) %all-gather.3.cloned.1.call-update) | async-done | bytes 2097168 | tf_op jit(solution)/shard_map/all_gather | solution.py:34
  63.7 17.4 %fusion.23 = f32[2048,256]{1,0:T(8,128)S(1)} fusion(f32[2048,256]{1,0:T(8,128)} %param.5, f32[1,2048,2048]{2,1,0:T(8,128)} %param.3, f32[1,2048,256]{1,2,0:T(8,128)} %all-gather.3.cloned.1.call-done), kind=kOutput, calls=%fused_computation.17 | convolution fusion | flops 12885426176 | bytes 23068672 | tf_op jit(solution)/shard_map/dot_general | solution.py:35
  81.1 31.3 %fusion.10 = f32[2048,256]{0,1:T(8,128)} fusion(f32[2048,256]{1,0:T(8,128)S(1)} %fusion.23, f32[1,2048,2048]{2,1,0:T(8,128)S(1)} %copy-done), kind=kOutput, calls=%fused_computation.10 | convolution fusion | flops 12884901888 | bytes 20971520 | tf_op jit(solution)/shard_map/dot_general | solution.py:38
  112.5 100.6 %all-reduce.7.cloned.1.call-done = f32[2048,256]{0,1:T(8,128)} async-done(((f32[2048,256]{0,1:T(8,128)}), f32[2048,256]{0,1:T(8,128)}) %all-reduce.7.cloned.1.call-update) | async-done | bytes 2097168 | tf_op jit(solution)/shard_map/psum | solution.py:38
  213.1 18.8 %fusion.13 = f32[2048,256]{0,1:T(8,128)} fusion(f32[1,2048,2048]{2,1,0:T(8,128)} %param.3, f32[1,2048,256]{1,2,0:T(8,128)S(1)} %copy-done.1, f32[2048,256]{0,1:T(8,128)} %all-reduce.7.cloned.1.call-done), kind=kOutput, calls=%fused_computation.11 | convolution fusion | flops 12885950464 | bytes 23068672 | tf_op jit(solution)/shard_map/dot_general | solution.py:40
  232.0 50.8 %all-reduce.9.cloned.1.call-done = f32[2048,256]{0,1:T(8,128)} async-done(((f32[2048,256]{0,1:T(8,128)}), f32[2048,256]{0,1:T(8,128)}) %all-reduce.9.cloned.1.call-update) | async-done | bytes 2097168 | tf_op jit(solution)/shard_map/psum | solution.py:41
  282.8 4.9 fusion.31
  287.7 71.2 %all-reduce.11.cloned.1.call-done = f32[256,256]{1,0:T(8,128)} async-done(((f32[256,256]{1,0:T(8,128)}), f32[256,256]{1,0:T(8,128)}) %all-reduce.11.cloned.1.call-update) | async-done | bytes 262160 | tf_op jit(solution)/shard_map/psum | solution.py:42
  358.9 1.6 multiply_reduce_fusion.1
  361.3 1.3 fusion.42
  362.8 1.3 fusion.49
  364.2 0.4 fusion.41
  364.5 0.4 fusion.57
  364.9 0.4 fusion.56
  365.3 0.4 fusion.40
  365.7 0.4 fusion.59
  366.1 0.4 fusion.58
  366.5 0.4 fusion.39
  366.9 0.4 fusion.61
  367.3 0.4 fusion.60
  367.6 0.4 fusion.38
  368.0 0.4 fusion.62
  368.5 4.4 fusion.22
  372.9 17.8 %fusion.16 = f32[2048,256]{0,1:T(8,128)} fusion(f32[2048,256]{0,1:T(8,128)S(1)} %fusion.22, f32[1,2048,2048]{2,1,0:T(8,128)} %param.3), kind=kOutput, calls=%fused_computation.12 | convolution fusion | flops 12884901888 | bytes 20971520 | tf_op jit(solution)/shard_map/dot_general | solution.py:38
  390.7 101.6 %all-reduce.13.cloned.1.call-done = f32[2048,256]{0,1:T(8,128)} async-done(((f32[2048,256]{0,1:T(8,128)}), f32[2048,256]{0,1:T(8,128)}) %all-reduce.13.cloned.1.call-update) | async-done | bytes 2097168 | tf_op jit(solution)/shard_map/psum | solution.py:38
  492.4 2.8 multiply_subtract_fusion
  495.2 1.3 copy-done.2
  496.5 17.9 %fusion.19 = f32[2048,256]{0,1:T(8,128)} fusion(f32[2048,256]{0,1:T(8,128)S(1)} %multiply_subtract_fusion, f32[1,2048,2048]{2,1,0:T(8,128)} %param.3), kind=kOutput, calls=%fused_computation.13 | convolution fusion | flops 12884901888 | bytes 20971520 | tf_op jit(solution)/shard_map/dot_general | solution.py:40
  514.7 50.6 %all-reduce.15.cloned.1.call-done = f32[2048,256]{0,1:T(8,128)} async-done(((f32[2048,256]{0,1:T(8,128)}), f32[2048,256]{0,1:T(8,128)}) %all-reduce.15.cloned.1.call-update) | async-done | bytes 2097168 | tf_op jit(solution)/shard_map/psum | solution.py:41
  565.2 4.9 fusion.28
  570.1 1.0 constant_dynamic-slice_fusion
  571.1 0.8 copy.7
  572.0 69.4 %all-reduce.17.cloned.1.call-done = f32[256,256]{1,0:T(8,128)} async-done(((f32[256,256]{1,0:T(8,128)}), f32[256,256]{1,0:T(8,128)}) %all-reduce.17.cloned.1.call-update) | async-done | bytes 262160 | tf_op jit(solution)/shard_map/psum | solution.py:42
  641.4 1.6 multiply_reduce_fusion
  643.7 1.3 fusion.37
  645.3 1.3 fusion.50
  646.6 0.4 fusion.36
  647.4 0.4 fusion.63
  647.8 0.4 fusion.35
  648.2 0.4 fusion.66
  648.6 0.4 fusion.65
  649.0 0.4 fusion.34
  649.3 0.4 fusion.68
  649.7 0.4 fusion.67
  650.2 0.4 fusion.33
  650.5 0.4 fusion.69
  651.0 4.8 convolution_multiply_fusion
  (24 shorter events, 1.6 us)
Async XLA Ops:
  7.2 56.5 %all-gather.3.cloned.1.call-start = ((), (), s32[]{:S(2)}) async-start(), calls=%async_computation.6 | async-start | bytes 2359296 | tf_op jit(solution)/shard_map/all_gather | solution.py:34
  9.0 204.1 %all-reduce.7.cloned.1.call-start = ((), (), s32[]{:S(2)}) async-start(), calls=%async_computation | async-start | bytes 4194304 | tf_op jit(solution)/shard_map/psum | solution.py:38
  63.7 17.4 %copy-start = (f32[1,2048,2048]{2,1,0:T(8,128)S(1)}, f32[1,2048,2048]{2,1,0:T(8,128)}, u32[]{:S(2)}) copy-start(f32[1,2048,2048]{2,1,0:T(8,128)} %param.3) | copy-start | bytes 50331652
  112.4 100.7 %copy-start.1 = (f32[1,2048,256]{1,2,0:T(8,128)S(1)}, f32[1,2048,256]{1,2,0:T(8,128)}, u32[]{:S(2)}) copy-start(f32[1,2048,256]{1,2,0:T(8,128)} %all-gather.3.cloned.1.call-done) | copy-start | bytes 6291460
  112.4 170.4 %all-reduce.9.cloned.1.call-start = ((), (), s32[]{:S(2)}) async-start(), calls=%async_computation.1 | async-start | bytes 4194304 | tf_op jit(solution)/shard_map/psum | solution.py:41
  231.9 127.0 %all-reduce.11.cloned.1.call-start = ((), (), s32[]{:S(2)}) async-start(), calls=%async_computation.2 | async-start | bytes 524288 | tf_op jit(solution)/shard_map/psum | solution.py:42
  287.7 204.7 %all-reduce.13.cloned.1.call-start = ((), (), s32[]{:S(2)}) async-start(), calls=%async_computation.3 | async-start | bytes 4194304 | tf_op jit(solution)/shard_map/psum | solution.py:38
  390.7 174.6 %all-reduce.15.cloned.1.call-start = ((), (), s32[]{:S(2)}) async-start(), calls=%async_computation.4 | async-start | bytes 4194304 | tf_op jit(solution)/shard_map/psum | solution.py:41
  495.2 1.3 copy-start.2
  514.4 127.0 %all-reduce.17.cloned.1.call-start = ((), (), s32[]{:S(2)}) async-start(), calls=%async_computation.5 | async-start | bytes 524288 | tf_op jit(solution)/shard_map/psum | solution.py:42
  648.9 2.0 copy-start.3
Sparse Core Ops, SparseCore 0:
  10.6 53.0 all-gather.2
  112.5 100.5 all-reduce.6
  232.1 50.6 all-reduce.8
  287.8 71.0 all-reduce.10
  390.8 101.5 all-reduce.12
  514.5 50.6 all-reduce.14
  570.3 71.0 all-reduce.16
where the time goes:
time: 667 us; the launch traced here: 663 us
  waiting for transfers between devices  499 us (75%)
  matrix products  136 us (20%)
  between operations  16.4 us (2%)
    psum x2, waiting for transfers between devices, local(): gradient = lax.psum(jnp.dot(samples.T, residual, precision=highest), 'row')  202 us
    psum x2, waiting for transfers between devices, local(): lax.psum(jnp.dot(average.T, average, precision=highest), 'row')  141 us
    psum x2, waiting for transfers between devices, local(): average = lax.psum(projected, 'view') / view_count  101 us
    all_gather x1, waiting for transfers between devices, local(): whole_map = lax.all_gather(map_shard, 'row', axis=0, tiled=True)  54.6 us
    dot_general x3, matrix products, local(): projected = jnp.dot(samples, whole_map, precision=highest)  54.1 us
    dot_general x2, matrix products, local(): gradient = lax.psum(jnp.dot(samples.T, residual, precision=highest), 'row')  49.1 us
  transfers between devices with their start and end apart: 7, of which 7 were waited for; matrix products, arithmetic and copies ran while one was open for 0% of the time, Pallas kernels for 0%

commit v1 on v0

--- a/solution.py
+++ b/solution.py
@@ -31,7 +31,12 @@
     total_rows = local_rows * lax.axis_size("row")
     view_count = lax.axis_size("view")
     step_size = step_rate * width / total_rows
-    whole_map = lax.all_gather(map_shard, "row", axis=0, tiled=True)
+    ring = [map_shard]
+    for hop in range(7):
+        ring.append(lax.ppermute(ring[-1], "row", [(dev, (dev + 1) % 8) for dev in range(8)]))
+    whole_map = jnp.roll(
+        jnp.concatenate(ring[::-1], axis=0), (lax.axis_index("row") + 1) * ring[0].shape[0], axis=0
+    )
     projected = jnp.dot(samples, whole_map, precision=highest)
     for iteration in range(ITERS):
         residual = projected - shared

time: 667 us -> 684 us (1.025)
  waiting for transfers between devices: 499 us -> 509 us
    ppermute x0 -> x7, waiting for transfers between devices: none -> 65.7 us  [local(): lax.ppermute(ring[-1], 'row', [(dev, (dev + 1) % 8) for dev in range(8)])]
    all_gather x1 -> x0, waiting for transfers between devices: 54.6 us -> none  [local(): whole_map = lax.all_gather(map_shard, 'row', axis=0, tiled=True)]
  transfers between devices with their start and end apart: 7 -> 13, of which waited for: 7 -> 13; matrix products, arithmetic and copies ran while one was open for 0% -> 0% of each run, Pallas kernels for 0% -> 0%
where the time goes in v1:
time: 684 us; the launch traced here: 678 us
  waiting for transfers between devices  509 us (74%)
  matrix products  137 us (20%)
  between operations  16.5 us (2%)
    psum x2, waiting for transfers between devices, local(): gradient = lax.psum(jnp.dot(samples.T, residual, precision=highest), 'row')  201 us
    psum x2, waiting for transfers between devices, local(): lax.psum(jnp.dot(average.T, average, precision=highest), 'row')  141 us
    psum x2, waiting for transfers between devices, local(): average = lax.psum(projected, 'view') / view_count  101 us
    ppermute x7, waiting for transfers between devices, local(): lax.ppermute(ring[-1], 'row', [(dev, (dev + 1) % 8) for dev in range(8)])  65.7 us
    dot_general x3, matrix products, local(): projected = jnp.dot(samples, whole_map, precision=highest)  55.9 us
    dot_general x2, matrix products, local(): gradient = lax.psum(jnp.dot(samples.T, residual, precision=highest), 'row')  49.1 us
  transfers between devices with their start and end apart: 13, of which 13 were waited for; matrix products, arithmetic and copies ran while one was open for 0% of the time, Pallas kernels for 0%

profile of v1, /device:TPU:0, one launch (start us, length us, event | category | flops | bytes accessed | tf_op | source)
XLA Modules:
  0.0 678.4 jit_solution(6600533347301761493)
XLA Ops:
  7.2 1.1 copy.6
  8.3 3.0 collective-permute-start
  11.3 9.3 %collective-permute-done = f32[256,256]{0,1:T(8,128)S(1)} collective-permute-done((f32[256,256]{0,1:T(8,128)S(1)}, f32[256,256]{0,1:T(8,128)S(1)}, u32[]{:S(2)}, u32[]{:S(2)}) %collective-permute-start) | collective-permute-done | bytes 262176 | tf_op jit(solution)/shard_map/ppermute | solution.py:36
  20.7 10.2 %collective-permute-done.1 = f32[256,256]{0,1:T(8,128)S(1)} collective-permute-done((f32[256,256]{0,1:T(8,128)S(1)}, f32[256,256]{0,1:T(8,128)S(1)}, u32[]{:S(2)}, u32[]{:S(2)}) %collective-permute-start.1) | collective-permute-done | bytes 262176 | tf_op jit(solution)/shard_map/ppermute | solution.py:36
  30.8 9.3 %collective-permute-done.2 = f32[256,256]{0,1:T(8,128)S(1)} collective-permute-done((f32[256,256]{0,1:T(8,128)S(1)}, f32[256,256]{0,1:T(8,128)S(1)}, u32[]{:S(2)}, u32[]{:S(2)}) %collective-permute-start.2) | collective-permute-done | bytes 262176 | tf_op jit(solution)/shard_map/ppermute | solution.py:36
  40.1 9.1 %collective-permute-done.3 = f32[256,256]{0,1:T(8,128)S(1)} collective-permute-done((f32[256,256]{0,1:T(8,128)S(1)}, f32[256,256]{0,1:T(8,128)S(1)}, u32[]{:S(2)}, u32[]{:S(2)}) %collective-permute-start.3) | collective-permute-done | bytes 262176 | tf_op jit(solution)/shard_map/ppermute | solution.py:36
  49.2 9.1 %collective-permute-done.4 = f32[256,256]{0,1:T(8,128)S(1)} collective-permute-done((f32[256,256]{0,1:T(8,128)S(1)}, f32[256,256]{0,1:T(8,128)S(1)}, u32[]{:S(2)}, u32[]{:S(2)}) %collective-permute-start.4) | collective-permute-done | bytes 262176 | tf_op jit(solution)/shard_map/ppermute | solution.py:36
  58.3 9.7 %collective-permute-done.5 = f32[256,256]{0,1:T(8,128)S(1)} collective-permute-done((f32[256,256]{0,1:T(8,128)S(1)}, f32[256,256]{0,1:T(8,128)S(1)}, u32[]{:S(2)}, u32[]{:S(2)}) %collective-permute-start.5) | collective-permute-done | bytes 262176 | tf_op jit(solution)/shard_map/ppermute | solution.py:36
  68.0 9.1 %collective-permute-done.6 = f32[256,256]{0,1:T(8,128)S(1)} collective-permute-done((f32[256,256]{0,1:T(8,128)S(1)}, f32[256,256]{0,1:T(8,128)S(1)}, u32[]{:S(2)}, u32[]{:S(2)}) %collective-permute-start.6) | collective-permute-done | bytes 262176 | tf_op jit(solution)/shard_map/ppermute | solution.py:36
  77.6 1.3 copy-done.5
  78.9 18.7 %fusion.26 = f32[2048,256]{1,0:T(8,128)S(1)} fusion(f32[2048,256]{1,0:T(8,128)S(1)} %copy-done.5, f32[1,2048,2048]{2,1,0:T(8,128)} %param.3, f32[4096,256]{0,1:T(8,128)S(1)} %constant_dynamic-update-slice_fusion, s32[]{:T(128)S(6)} %select_n.17), kind=kOutput, calls=%fused_computation.18 | convolution fusion | flops 12885426176 | bytes 23068676 | tf_op jit(solution)/shard_map/dot_general | solution.py:40
  97.6 31.3 %fusion.13 = f32[2048,256]{0,1:T(8,128)} fusion(f32[2048,256]{1,0:T(8,128)S(1)} %fusion.26, f32[1,2048,2048]{2,1,0:T(8,128)S(1)} %bitcast.93), kind=kOutput, calls=%fused_computation.11 | convolution fusion | flops 12884901888 | bytes 20971520 | tf_op jit(solution)/shard_map/dot_general | solution.py:43
  129.1 99.5 %all-reduce.7.cloned.1.call-done = f32[2048,256]{0,1:T(8,128)} async-done(((f32[2048,256]{0,1:T(8,128)}), f32[2048,256]{0,1:T(8,128)}) %all-reduce.7.cloned.1.call-update) | async-done | bytes 2097168 | tf_op jit(solution)/shard_map/psum | solution.py:43
  228.6 19.4 %fusion.16 = f32[2048,256]{0,1:T(8,128)} fusion(f32[1,2048,2048]{2,1,0:T(8,128)} %param.3, f32[2048,256]{0,1:T(8,128)} %all-reduce.7.cloned.1.call-done, f32[4096,256]{0,1:T(8,128)} %copy-done.3, s32[]{:T(128)S(6)} %select_n.17), kind=kOutput, calls=%fused_computation.12 | convolution fusion | flops 12885950464 | bytes 23068676 | tf_op jit(solution)/shard_map/dot_general | solution.py:45
  248.1 50.8 %all-reduce.9.cloned.1.call-done = f32[2048,256]{0,1:T(8,128)} async-done(((f32[2048,256]{0,1:T(8,128)}), f32[2048,256]{0,1:T(8,128)}) %all-reduce.9.cloned.1.call-update) | async-done | bytes 2097168 | tf_op jit(solution)/shard_map/psum | solution.py:46
  298.8 4.9 fusion.33
  303.8 71.2 %all-reduce.11.cloned.1.call-done = f32[256,256]{1,0:T(8,128)} async-done(((f32[256,256]{1,0:T(8,128)}), f32[256,256]{1,0:T(8,128)}) %all-reduce.11.cloned.1.call-update) | async-done | bytes 262160 | tf_op jit(solution)/shard_map/psum | solution.py:47
  375.0 1.6 multiply_reduce_fusion.1
  377.3 1.3 fusion.45
  378.9 1.3 fusion.52
  380.2 0.4 fusion.44
  381.4 0.4 fusion.43
  382.5 0.4 fusion.42
  383.3 0.4 fusion.66
  383.8 0.4 fusion.41
  384.6 3.7 fusion.25
  388.3 17.8 %fusion.19 = f32[2048,256]{0,1:T(8,128)} fusion(f32[2048,256]{0,1:T(8,128)S(1)} %fusion.25, f32[1,2048,2048]{2,1,0:T(8,128)} %param.3), kind=kOutput, calls=%fused_computation.13 | convolution fusion | flops 12884901888 | bytes 20971520 | tf_op jit(solution)/shard_map/dot_general | solution.py:43
  406.2 101.6 %all-reduce.13.cloned.1.call-done = f32[2048,256]{0,1:T(8,128)} async-done(((f32[2048,256]{0,1:T(8,128)}), f32[2048,256]{0,1:T(8,128)}) %all-reduce.13.cloned.1.call-update) | async-done | bytes 2097168 | tf_op jit(solution)/shard_map/psum | solution.py:43
  507.8 2.8 multiply_subtract_fusion
  510.7 1.3 copy-done.2
  512.0 17.8 %fusion.22 = f32[2048,256]{0,1:T(8,128)} fusion(f32[2048,256]{0,1:T(8,128)S(1)} %multiply_subtract_fusion, f32[1,2048,2048]{2,1,0:T(8,128)} %param.3), kind=kOutput, calls=%fused_computation.14 | convolution fusion | flops 12884901888 | bytes 20971520 | tf_op jit(solution)/shard_map/dot_general | solution.py:45
  530.1 50.6 %all-reduce.15.cloned.1.call-done = f32[2048,256]{0,1:T(8,128)} async-done(((f32[2048,256]{0,1:T(8,128)}), f32[2048,256]{0,1:T(8,128)}) %all-reduce.15.cloned.1.call-update) | async-done | bytes 2097168 | tf_op jit(solution)/shard_map/psum | solution.py:46
  580.6 4.9 fusion.30
  585.5 1.0 constant_dynamic-slice_fusion
  586.5 0.8 copy.7
  587.4 69.4 %all-reduce.17.cloned.1.call-done = f32[256,256]{1,0:T(8,128)} async-done(((f32[256,256]{1,0:T(8,128)}), f32[256,256]{1,0:T(8,128)}) %all-reduce.17.cloned.1.call-update) | async-done | bytes 262160 | tf_op jit(solution)/shard_map/psum | solution.py:47
  656.8 1.6 multiply_reduce_fusion
  659.2 1.3 fusion.40
  660.7 1.3 fusion.53
  662.1 0.4 fusion.39
  663.2 0.4 fusion.38
  663.6 0.4 fusion.71
  664.0 0.4 fusion.70
  664.4 0.4 fusion.37
  665.2 0.4 fusion.73
  665.6 0.4 fusion.36
  666.0 0.4 fusion.74
  666.4 4.8 convolution_multiply_fusion
  (64 shorter events, 5.0 us)
Async XLA Ops:
  7.2 221.4 %all-reduce.7.cloned.1.call-start = ((), (), s32[]{:S(2)}) async-start(), calls=%async_computation | async-start | bytes 4194304 | tf_op jit(solution)/shard_map/psum | solution.py:43
  8.3 12.4 %collective-permute-start = (f32[256,256]{0,1:T(8,128)S(1)}, f32[256,256]{0,1:T(8,128)S(1)}, u32[]{:S(2)}, u32[]{:S(2)}) collective-permute-start(f32[256,256]{0,1:T(8,128)S(1)} %bitcast.94), channel_id=1, source_target_pairs={{0,1},{1,2},{2,3},{3,4},{4,5},{5,6},{6,7},{7,0},{8,9},{9,10},{10,1... | collective-permute-start | bytes 786440 | tf_op jit(solution)/shard_map/ppermute | solution.py:36
  20.7 10.2 %collective-permute-start.1 = (f32[256,256]{0,1:T(8,128)S(1)}, f32[256,256]{0,1:T(8,128)S(1)}, u32[]{:S(2)}, u32[]{:S(2)}) collective-permute-start(f32[256,256]{0,1:T(8,128)S(1)} %collective-permute-done), channel_id=1, source_target_pairs={{0,1},{1,2},{2,3},{3,4},{4,5},{5,6},{6,7},{7,0},{8,9},{9,10},{10,1... | collective-permute-start | bytes 786440 | tf_op jit(solution)/shard_map/ppermute | solution.py:36
  30.8 9.3 %collective-permute-start.2 = (f32[256,256]{0,1:T(8,128)S(1)}, f32[256,256]{0,1:T(8,128)S(1)}, u32[]{:S(2)}, u32[]{:S(2)}) collective-permute-start(f32[256,256]{0,1:T(8,128)S(1)} %collective-permute-done.1), channel_id=1, source_target_pairs={{0,1},{1,2},{2,3},{3,4},{4,5},{5,6},{6,7},{7,0},{8,9},{9,10},{10,1... | collective-permute-start | bytes 786440 | tf_op jit(solution)/shard_map/ppermute | solution.py:36
  40.1 9.1 %collective-permute-start.3 = (f32[256,256]{0,1:T(8,128)S(1)}, f32[256,256]{0,1:T(8,128)S(1)}, u32[]{:S(2)}, u32[]{:S(2)}) collective-permute-start(f32[256,256]{0,1:T(8,128)S(1)} %collective-permute-done.2), channel_id=1, source_target_pairs={{0,1},{1,2},{2,3},{3,4},{4,5},{5,6},{6,7},{7,0},{8,9},{9,10},{10,1... | collective-permute-start | bytes 786440 | tf_op jit(solution)/shard_map/ppermute | solution.py:36
  49.2 9.1 %collective-permute-start.4 = (f32[256,256]{0,1:T(8,128)S(1)}, f32[256,256]{0,1:T(8,128)S(1)}, u32[]{:S(2)}, u32[]{:S(2)}) collective-permute-start(f32[256,256]{0,1:T(8,128)S(1)} %collective-permute-done.3), channel_id=1, source_target_pairs={{0,1},{1,2},{2,3},{3,4},{4,5},{5,6},{6,7},{7,0},{8,9},{9,10},{10,1... | collective-permute-start | bytes 786440 | tf_op jit(solution)/shard_map/ppermute | solution.py:36
  58.3 9.7 %collective-permute-start.5 = (f32[256,256]{0,1:T(8,128)S(1)}, f32[256,256]{0,1:T(8,128)S(1)}, u32[]{:S(2)}, u32[]{:S(2)}) collective-permute-start(f32[256,256]{0,1:T(8,128)S(1)} %collective-permute-done.4), channel_id=1, source_target_pairs={{0,1},{1,2},{2,3},{3,4},{4,5},{5,6},{6,7},{7,0},{8,9},{9,10},{10,1... | collective-permute-start | bytes 786440 | tf_op jit(solution)/shard_map/ppermute | solution.py:36
  68.0 9.1 %collective-permute-start.6 = (f32[256,256]{0,1:T(8,128)S(1)}, f32[256,256]{0,1:T(8,128)S(1)}, u32[]{:S(2)}, u32[]{:S(2)}) collective-permute-start(f32[256,256]{0,1:T(8,128)S(1)} %collective-permute-done.5), channel_id=1, source_target_pairs={{0,1},{1,2},{2,3},{3,4},{4,5},{5,6},{6,7},{7,0},{8,9},{9,10},{10,1... | collective-permute-start | bytes 786440 | tf_op jit(solution)/shard_map/ppermute | solution.py:36
  77.3 1.6 copy-start.5
  77.6 20.0 %slice-start = ((s8[16777216]{0:T(1024)(128)(4,1)}), s8[4194304]{0:T(1024)(128)(4,1)S(1)}, s32[]{:S(2)}) async-start(s8[16777216]{0:T(1024)(128)(4,1)} %bitcast.92), calls=%async_computation.6 | async-start | bytes 8388608
  78.9 18.7 %copy-start.3 = (f32[4096,256]{0,1:T(8,128)}, f32[4096,256]{0,1:T(8,128)S(1)}, u32[]{:S(2)}) copy-start(f32[4096,256]{0,1:T(8,128)S(1)} %constant_dynamic-update-slice_fusion) | copy-start | bytes 12582916
  78.9 18.7 %slice-start.1 = ((s8[16777216]{0:T(1024)(128)(4,1)}), s8[4194304]{0:T(1024)(128)(4,1)S(1)}, s32[]{:S(2)}) async-start(s8[16777216]{0:T(1024)(128)(4,1)} %bitcast.92), calls=%async_computation.7 | async-start | bytes 8388608
  78.9 18.7 %slice-start.2 = ((s8[16777216]{0:T(1024)(128)(4,1)}), s8[4194304]{0:T(1024)(128)(4,1)S(1)}, s32[]{:S(2)}) async-start(s8[16777216]{0:T(1024)(128)(4,1)} %bitcast.92), calls=%async_computation.8 | async-start | bytes 8388608
  78.9 18.7 %slice-start.3 = ((s8[16777216]{0:T(1024)(128)(4,1)}), s8[4194304]{0:T(1024)(128)(4,1)S(1)}, s32[]{:S(2)}) async-start(s8[16777216]{0:T(1024)(128)(4,1)} %bitcast.92), calls=%async_computation.9 | async-start | bytes 8388608
  129.0 169.8 %all-reduce.9.cloned.1.call-start = ((), (), s32[]{:S(2)}) async-start(), calls=%async_computation.1 | async-start | bytes 4194304 | tf_op jit(solution)/shard_map/psum | solution.py:46
  248.0 127.0 %all-reduce.11.cloned.1.call-start = ((), (), s32[]{:S(2)}) async-start(), calls=%async_computation.2 | async-start | bytes 524288 | tf_op jit(solution)/shard_map/psum | solution.py:47
  303.7 204.1 %all-reduce.13.cloned.1.call-start = ((), (), s32[]{:S(2)}) async-start(), calls=%async_computation.3 | async-start | bytes 4194304 | tf_op jit(solution)/shard_map/psum | solution.py:43
  382.5 2.0 copy-start
  406.1 101.7 %copy-start.1 = (f32[2048,256]{0,1:T(8,128)S(1)}, f32[2048,256]{0,1:T(8,128)}, u32[]{:S(2)}) copy-start(f32[2048,256]{0,1:T(8,128)} %all-reduce.7.cloned.1.call-done) | copy-start | bytes 6291460
  406.1 174.5 %all-reduce.15.cloned.1.call-start = ((), (), s32[]{:S(2)}) async-start(), calls=%async_computation.4 | async-start | bytes 4194304 | tf_op jit(solution)/shard_map/psum | solution.py:46
  510.7 1.3 copy-start.2
  529.8 127.0 %all-reduce.17.cloned.1.call-start = ((), (), s32[]{:S(2)}) async-start(), calls=%async_computation.5 | async-start | bytes 524288 | tf_op jit(solution)/shard_map/psum | solution.py:47
  664.4 2.0 copy-start.4
Sparse Core Ops, SparseCore 0:
  129.1 99.3 all-reduce.6
  248.1 50.6 all-reduce.8
  303.8 71.0 all-reduce.10
  406.2 101.5 all-reduce.12
  529.9 50.6 all-reduce.14
  585.7 71.0 all-reduce.16
